TPU v7x, 32 devices: a whole 2x2x4 slice. The times are simulated.
32 devices in a mesh: pipe: 2 (over core), grp: 4 (over z), dp: 4 (over y, x).
Axes of the slice: x: 2, y: 2, z: 4, core: 2. Of those that a mesh axis runs over, the one named last changes fastest.
Arguments:
- block_input: bfloat16 [2, 16, 512, 512], P(None, ('grp', 'dp')), may hold values from -6 to 6
- cotangent: bfloat16 [2, 16, 512, 512], P(None, ('grp', 'dp')), may hold values from -6 to 6
- segments: int32 [2, 16, 512], P(None, ('grp', 'dp')), may hold values from 0 to 7, never falling along the last dimension, each value on 1 to 256 neighbouring positions
- ln1_gain: float32 [2, 512], P('pipe'), may hold values from 0.5 to 1.5
- ln1_shift: float32 [2, 512], P('pipe'), may hold values from -1.25 to 1.25
- qkv_weight: bfloat16 [2, 512, 1536], P('pipe'), may hold values from -0.25 to 0.25
- qkv_bias: float32 [2, 1536], P('pipe'), may hold values from -1.25 to 1.25
- attn_weight: bfloat16 [2, 512, 512], P('pipe'), may hold values from -1.5 to 1.5
- attn_bias: float32 [2, 512], P('pipe'), may hold values from -1.25 to 1.25
- ln2_gain: float32 [2, 512], P('pipe'), may hold values from 0.5 to 1.5
- ln2_shift: float32 [2, 512], P('pipe'), may hold values from -1.25 to 1.25
- ff_in_weight: bfloat16 [2, 512, 2048], P('pipe'), may hold values from -0.25 to 0.25
- ff_in_bias: float32 [2, 2048], P('pipe'), may hold values from -1.25 to 1.25
- ff_out_weight: bfloat16 [2, 2048, 512], P('pipe'), may hold values from -0.125 to 0.125
- ff_out_bias: float32 [2, 512], P('pipe'), may hold values from -1.25 to 1.25
- prefix_embed: float32 [10, 512], replicated, may hold values from -6 to 6
- up_weight: float32 [512, 512], replicated, may hold values from -0.25 to 0.25
- up_bias: float32 [512], replicated, may hold values from -3 to 3
- out_weight: float32 [512, 2048], replicated, may hold values from -0.375 to 0.375
- out_bias: float32 [2048], replicated, may hold values from -1.75 to 1.75
Outputs:
- activations: bfloat16 [2, 2, 16, 512, 512], P('pipe', None, ('grp', 'dp'))
- input_grads: float32 [2, 2, 16, 512, 512], P('pipe', None, ('grp', 'dp'))
- grad_embed: float32 [10, 512], replicated
- grad_up_weight: float32 [512, 512], replicated
- grad_up_bias: float32 [512], replicated
- grad_out_weight: float32 [512, 2048], P(None, ('pipe', 'dp'))
- grad_out_bias: float32 [2048], P(('pipe', 'dp'))
Inputs may be any that keep to these rules, and one draw needn't show every extreme that they name: `segments`: within a packed row segment numbers never fall, and every segment holds 1 to 256 tokens.
All inputs are finite; a program needn't handle non-finite values.
Results may differ from a plain program's by a relative error of at most 0.019.
Values may be sent and summed in bfloat16 or wider, within the bound.
No kernel may reach another device: no remote copies, remote signals or barrier semaphores. Data moves between devices by JAX's collectives and lax.ppermute only.
A program may use at most 192 MiB of HBM per device.

v0:
```python
from functools import partial
import math
import jax
import jax.numpy as jnp
from jax import lax
from jax.sharding import PartitionSpec as P

D = 512
HEADS = 8
HD = 64
FF = 2048
ROT = 16
PREFIX = 10


def passed_along(shard, axis, by):
    peers = lax.axis_size(axis)
    pairs = [(i, i + by) for i in range(peers) if 0 <= i + by < peers]
    return lax.ppermute(shard, axis, pairs)


def matmul_hi(left_mat, right_mat):
    return jnp.dot(
        left_mat, right_mat, precision=lax.Precision.HIGHEST, preferred_element_type=jnp.float32
    )


def layer_norm(values, gain_vec, shift_vec):
    row_mean = jnp.mean(values, axis=-1, keepdims=True)
    centered = values - row_mean
    variance = jnp.mean(centered * centered, axis=-1, keepdims=True)
    return centered * lax.rsqrt(variance + 1e-05) * gain_vec + shift_vec


def rotate_heads(head_rows):
    half_rot = ROT // 2
    positions = jnp.arange(head_rows.shape[0]).astype(head_rows.dtype)
    inv_freq = jnp.exp(
        jnp.arange(half_rot).astype(head_rows.dtype) * (-2.0 * math.log(10000.0) / ROT)
    )
    angles = positions[:, None] * inv_freq[None, :]
    cosine = jnp.cos(angles)[:, None, :]
    sine_val = jnp.sin(angles)[:, None, :]
    lead_part = head_rows[..., :half_rot]
    tail_part = head_rows[..., half_rot:ROT]
    return jnp.concatenate(
        [
            lead_part * cosine - tail_part * sine_val,
            tail_part * cosine + lead_part * sine_val,
            head_rows[..., ROT:],
        ],
        axis=-1,
    )


def block_mask(seg_row, row_start, block_rows):
    query_pos = row_start + jnp.arange(block_rows)
    key_pos = jnp.arange(seg_row.shape[0])
    seg_query = seg_row[row_start : row_start + block_rows]
    inner_mask = (key_pos[None, :] <= query_pos[:, None]) & (seg_row[None, :] == seg_query[:, None])
    return jnp.concatenate([jnp.ones((block_rows, PREFIX), dtype=jnp.bool_), inner_mask], axis=1)


def attention_forward(queries, key_list, value_list, seg_row):
    seq_len = queries.shape[0]
    block_rows = min(512, seq_len)
    scores = jnp.einsum(
        "qhd,khd->hqk", queries, key_list, preferred_element_type=jnp.float32
    ) * HD ** (-0.5)
    scores = jnp.where(block_mask(seg_row, 0, block_rows)[None], scores, -1e30)
    row_peak = jnp.max(scores, axis=-1, keepdims=True)
    exponent = jnp.exp(scores - row_peak)
    row_total = jnp.sum(exponent, axis=-1, keepdims=True)
    probs_low = (exponent / row_total).astype(jnp.bfloat16)
    outputs = [
        jnp.einsum(
            "hqk,khd->qhd", probs_low, value_list, preferred_element_type=jnp.float32
        ).astype(jnp.bfloat16)
    ]
    totals = [(row_peak + jnp.log(row_total))[..., 0]]
    return (jnp.concatenate(outputs, axis=0), jnp.concatenate(totals, axis=1))


def attention_backward(queries, key_list, value_list, log_totals, grad_mixed, seg_row):
    seq_len = queries.shape[0]
    block_rows = min(512, seq_len)
    grad_keys = jnp.zeros(key_list.shape, jnp.float32)
    grad_values = jnp.zeros(value_list.shape, jnp.float32)
    grad_query_parts = []
    for row_start in range(0, seq_len, block_rows):
        query_block = queries[row_start : row_start + block_rows]
        grad_block = grad_mixed[row_start : row_start + block_rows]
        allowed = block_mask(seg_row, row_start, block_rows)[None]
        scores = jnp.einsum(
            "qhd,khd->hqk", query_block, key_list, preferred_element_type=jnp.float32
        ) * HD ** (-0.5)
        block_lse = log_totals[:, row_start : row_start + block_rows][:, :, None]
        probs_full = jnp.where(allowed, jnp.exp(scores - block_lse), 0.0)
        probs_low = probs_full.astype(jnp.bfloat16)
        grad_values = grad_values + jnp.einsum(
            "hqk,qhd->khd", probs_low, grad_block, preferred_element_type=jnp.float32
        )
        grad_probs = jnp.einsum(
            "qhd,khd->hqk", grad_block, value_list, preferred_element_type=jnp.float32
        )
        inner_sum = jnp.sum(probs_full * grad_probs, axis=-1, keepdims=True)
        grad_scores = (probs_full * (grad_probs - inner_sum)).astype(jnp.bfloat16)
        grad_query_parts.append(
            jnp.einsum("hqk,khd->qhd", grad_scores, key_list, preferred_element_type=jnp.float32)
            * HD ** (-0.5)
        )
        grad_keys = grad_keys + jnp.einsum(
            "hqk,qhd->khd", grad_scores, query_block, preferred_element_type=jnp.float32
        ) * HD ** (-0.5)
    return (jnp.concatenate(grad_query_parts, axis=0), grad_keys, grad_values)


def forward_layer(row_in, seg_row, prefix_keys, prefix_values, params):
    (
        gain_one,
        shift_one,
        w_qkv,
        b_qkv,
        w_attn,
        b_attn,
        gain_two,
        shift_two,
        w_in,
        bias_in,
        w_back,
        bias_back,
    ) = params
    seq_len = row_in.shape[0]
    hidden = row_in.astype(jnp.float32)
    normed_one = layer_norm(hidden, gain_one, shift_one).astype(jnp.bfloat16)
    packed = jnp.dot(normed_one, w_qkv, preferred_element_type=jnp.float32) + b_qkv
    queries = rotate_heads(packed[:, :D].reshape(seq_len, HEADS, HD)).astype(jnp.bfloat16)
    key_rows = rotate_heads(packed[:, D : 2 * D].reshape(seq_len, HEADS, HD)).astype(jnp.bfloat16)
    value_rows = packed[:, 2 * D :].reshape(seq_len, HEADS, HD).astype(jnp.bfloat16)
    key_list = jnp.concatenate([prefix_keys, key_rows], axis=0)
    value_list = jnp.concatenate([prefix_values, value_rows], axis=0)
    mixed_heads, log_totals = attention_forward(queries, key_list, value_list, seg_row)
    attn_out = (
        jnp.dot(mixed_heads.reshape(seq_len, D), w_attn, preferred_element_type=jnp.float32)
        + b_attn
    )
    normed_two = layer_norm(hidden, gain_two, shift_two).astype(jnp.bfloat16)
    before = jnp.dot(normed_two, w_in, preferred_element_type=jnp.float32) + bias_in
    activated = jax.nn.gelu(before, approximate=False).astype(jnp.bfloat16)
    result = (
        hidden
        + attn_out
        + jnp.dot(activated, w_back, preferred_element_type=jnp.float32)
        + bias_back
    )
    return (result.astype(jnp.bfloat16), (queries, key_rows, value_rows, log_totals, before))


def backward_layer(grad_out, row_in, seg_row, prefix_keys, prefix_values, kept_state, params):
    (
        gain_one,
        shift_one,
        w_qkv,
        b_qkv,
        w_attn,
        b_attn,
        gain_two,
        shift_two,
        w_in,
        bias_in,
        w_back,
        bias_back,
    ) = params
    queries, key_rows, value_rows, log_totals, before = kept_state
    seq_len = row_in.shape[0]
    hidden = row_in.astype(jnp.float32)
    grad_activated = jnp.dot(grad_out, w_back.T, preferred_element_type=jnp.float32)
    gelu_back = jax.vjp(partial(jax.nn.gelu, approximate=False), before)[1]
    grad_before = gelu_back(grad_activated)[0].astype(jnp.bfloat16)
    grad_normed_two = jnp.dot(grad_before, w_in.T, preferred_element_type=jnp.float32)
    norm_two_back = jax.vjp(partial(layer_norm, gain_vec=gain_two, shift_vec=shift_two), hidden)[1]
    grad_mixed = (
        jnp.dot(grad_out, w_attn.T, preferred_element_type=jnp.float32)
        .astype(jnp.bfloat16)
        .reshape(seq_len, HEADS, HD)
    )
    key_list = jnp.concatenate([prefix_keys, key_rows], axis=0)
    value_list = jnp.concatenate([prefix_values, value_rows], axis=0)
    grad_queries, grad_keys, grad_values = attention_backward(
        queries, key_list, value_list, log_totals, grad_mixed, seg_row
    )
    grad_q_raw = jax.vjp(rotate_heads, grad_queries)[1](grad_queries)[0]
    grad_key_part = grad_keys[PREFIX:]
    grad_k_raw = jax.vjp(rotate_heads, grad_key_part)[1](grad_key_part)[0]
    grad_packed = jnp.concatenate(
        [
            grad_q_raw.reshape(seq_len, D),
            grad_k_raw.reshape(seq_len, D),
            grad_values[PREFIX:].reshape(seq_len, D),
        ],
        axis=1,
    ).astype(jnp.bfloat16)
    grad_normed_one = jnp.dot(grad_packed, w_qkv.T, preferred_element_type=jnp.float32)
    norm_one_back = jax.vjp(partial(layer_norm, gain_vec=gain_one, shift_vec=shift_one), hidden)[1]
    grad_in = (
        grad_out.astype(jnp.float32)
        + norm_two_back(grad_normed_two)[0]
        + norm_one_back(grad_normed_one)[0]
    )
    prefix_grad = jnp.concatenate(
        [grad_keys[:PREFIX].reshape(PREFIX, D), grad_values[:PREFIX].reshape(PREFIX, D)], axis=1
    )
    return (grad_in, prefix_grad)


def local(
    block_input,
    cotangent,
    segments,
    ln1_gain,
    ln1_shift,
    qkv_weight,
    qkv_bias,
    attn_weight,
    attn_bias,
    ln2_gain,
    ln2_shift,
    ff_in_weight,
    ff_in_bias,
    ff_out_weight,
    ff_out_bias,
    prefix_embed,
    up_weight,
    up_bias,
    out_weight,
    out_bias,
):
    section_id = lax.axis_index("pipe")
    micro_count = block_input.shape[0]
    seq_len = block_input.shape[2]
    hidden_units = jnp.tanh(matmul_hi(prefix_embed, up_weight) + up_bias)
    prefix_states = matmul_hi(hidden_units, out_weight) + out_bias
    seg_rows = segments[:, 0]
    params = tuple(
        (
            array_in[0]
            for array_in in (
                ln1_gain,
                ln1_shift,
                qkv_weight,
                qkv_bias,
                attn_weight,
                attn_bias,
                ln2_gain,
                ln2_shift,
                ff_in_weight,
                ff_in_bias,
                ff_out_weight,
                ff_out_bias,
            )
        )
    )
    section_states = lax.dynamic_slice_in_dim(prefix_states, section_id * (2 * D), 2 * D, 1).astype(
        jnp.bfloat16
    )
    prefix_keys = section_states[:, :D].reshape(PREFIX, HEADS, HD)
    prefix_values = section_states[:, D:].reshape(PREFIX, HEADS, HD)

    def run_full(row_in, seg_row):
        return forward_layer(row_in, seg_row, prefix_keys, prefix_values, params)

    def skip_full(row_in, seg_row):
        return (
            jnp.zeros((seq_len, D), jnp.bfloat16),
            (
                jnp.zeros((seq_len, HEADS, HD), jnp.bfloat16),
                jnp.zeros((seq_len, HEADS, HD), jnp.bfloat16),
                jnp.zeros((seq_len, HEADS, HD), jnp.bfloat16),
                jnp.zeros((HEADS, seq_len), jnp.float32),
                jnp.zeros((seq_len, FF), jnp.float32),
            ),
        )

    received = jnp.zeros((seq_len, D), jnp.bfloat16)
    tick_inputs = []
    tick_outputs = []
    tick_kept = []
    for tick_num in range(micro_count + 1):
        micro_idx = tick_num - section_id
        active = (micro_idx >= 0) & (micro_idx < micro_count)
        clamped = jnp.clip(micro_idx, 0, micro_count - 1)
        own_row = block_input[min(tick_num, micro_count - 1), 0]
        row_in = jnp.where(section_id == 0, own_row, received)
        seg_row = lax.dynamic_index_in_dim(seg_rows, clamped, 0, keepdims=False)
        result, kept_state = lax.cond(active, run_full, skip_full, row_in, seg_row)
        tick_kept.append(kept_state)
        tick_inputs.append(row_in)
        tick_outputs.append(result)
        if tick_num < micro_count:
            received = passed_along(result, "pipe", 1)

    def by_section(early_val, later_val):
        return jnp.where(section_id == 0, early_val, later_val)

    inputs_by_micro = jnp.stack(
        [
            by_section(tick_inputs[micro_num], tick_inputs[micro_num + 1])
            for micro_num in range(micro_count)
        ]
    )
    outputs_by_micro = jnp.stack(
        [
            by_section(tick_outputs[micro_num], tick_outputs[micro_num + 1])
            for micro_num in range(micro_count)
        ]
    )
    kept_by_micro = jax.tree.map(
        lambda *leaf_list: jnp.stack(leaf_list),
        *[
            jax.tree.map(by_section, tick_kept[micro_num], tick_kept[micro_num + 1])
            for micro_num in range(micro_count)
        ]
    )

    def back_kept(grad_out, row_in, seg_row, kept_state):
        return backward_layer(
            grad_out, row_in, seg_row, prefix_keys, prefix_values, kept_state, params
        )

    def skip_kept(grad_out, row_in, seg_row, kept_state):
        return (jnp.zeros((seq_len, D), jnp.float32), jnp.zeros((PREFIX, 2 * D), jnp.float32))

    received_grad = jnp.zeros((seq_len, D), jnp.bfloat16)
    prefix_total = jnp.zeros((PREFIX, 2 * D), jnp.float32)
    tick_grads = []
    for tick_num in range(micro_count + 1):
        micro_idx = tick_num - 1 + section_id
        active = (micro_idx >= 0) & (micro_idx < micro_count)
        clamped = jnp.clip(micro_idx, 0, micro_count - 1)
        own_cot = cotangent[min(tick_num, micro_count - 1), 0]
        grad_out = jnp.where(section_id == 1, own_cot, received_grad)
        row_in = lax.dynamic_index_in_dim(inputs_by_micro, clamped, 0, keepdims=False)
        seg_row = lax.dynamic_index_in_dim(seg_rows, clamped, 0, keepdims=False)
        kept_state = jax.tree.map(
            partial(lax.dynamic_index_in_dim, index=clamped, axis=0, keepdims=False), kept_by_micro
        )
        grad_in, prefix_grad = lax.cond(
            active, back_kept, skip_kept, grad_out, row_in, seg_row, kept_state
        )
        prefix_total = prefix_total + prefix_grad
        tick_grads.append(grad_in)
        if tick_num < micro_count:
            received_grad = passed_along(grad_in.astype(jnp.bfloat16), "pipe", -1)
    grads_by_micro = jnp.stack(
        [
            jnp.where(section_id == 1, tick_grads[micro_num], tick_grads[micro_num + 1])
            for micro_num in range(micro_count)
        ]
    )
    dp_index = lax.axis_index("dp")
    col_width = 2 * D // lax.axis_size("dp")
    local_cols = lax.psum_scatter(prefix_total, "dp", scatter_dimension=1, tiled=True)
    local_cols = lax.psum(local_cols, "grp")
    grad_out_weight = matmul_hi(hidden_units.T, local_cols)
    grad_out_bias = jnp.sum(local_cols, axis=0)
    out_cols = lax.dynamic_slice_in_dim(
        out_weight, section_id * (2 * D) + dp_index * col_width, col_width, 1
    )
    hidden_part = matmul_hi(local_cols, out_cols.T)
    hidden_grad = lax.psum(hidden_part, ("pipe", "dp"))
    grad_pre = hidden_grad * (1.0 - hidden_units * hidden_units)
    grad_up_weight = matmul_hi(prefix_embed.T, grad_pre)
    grad_up_bias = jnp.sum(grad_pre, axis=0)
    grad_embed = matmul_hi(grad_pre, up_weight.T)
    activations = outputs_by_micro[None, :, None]
    input_grads = grads_by_micro[None, :, None]
    return (
        activations,
        input_grads,
        grad_embed,
        grad_up_weight,
        grad_up_bias,
        grad_out_weight,
        grad_out_bias,
    )


def solution(mesh):
    return jax.shard_map(
        local,
        mesh=mesh,
        in_specs=(
            P(None, ("grp", "dp"), None, None),
            P(None, ("grp", "dp"), None, None),
            P(None, ("grp", "dp"), None),
            P("pipe", None),
            P("pipe", None),
            P("pipe", None, None),
            P("pipe", None),
            P("pipe", None, None),
            P("pipe", None),
            P("pipe", None),
            P("pipe", None),
            P("pipe", None, None),
            P("pipe", None),
            P("pipe", None, None),
            P("pipe", None),
            P(),
            P(),
            P(),
            P(),
            P(),
        ),
        out_specs=(
            P("pipe", None, ("grp", "dp"), None, None),
            P("pipe", None, ("grp", "dp"), None, None),
            P(),
            P(),
            P(),
            P(None, ("pipe", "dp")),
            P(("pipe", "dp")),
        ),
        check_vma=False,
    )
```

profile of v0, /device:TPU:1, one launch (start us, length us, event | category | flops | bytes accessed | tf_op | source)
XLA Modules:
  0.0 516.9 jit_solution(15525232900893411581)
XLA Ops:
  10.4 4.3 fusion.604
  16.2 14.4 %conditional.6 = (bf16[512,512]{1,0:T(8,128)(2,1)}, bf16[512,8,64]{0,2,1:T(8,128)(2,1)}, bf16[512,8,64]{0,2,1:T(8,128)(2,1)}, bf16[512,8,64]{0,2,1:T(8,128)(2,1)...) conditional(s32[]{:T(128)} %convert_element_type.537, () %tuple.74, (bf16[512,512]{1,0:T(8,128)(2,1)S(1)}, ...), branch_computations={%region_0.1_spmd, %region_1.6_spmd} | conditional | flops 3878450176 | bytes 134584976 | solution.py:295
  31.9 41.8 %collective-permute-done = bf16[512,512]{1,0:T(8,128)(2,1)} collective-permute-done((bf16[512,512]{1,0:T(8,128)(2,1)}, bf16[512,512]{1,0:T(8,128)(2,1)}, u32[]{:S(2)}, u32[]{:S(2)}) %collective-permute-start) | collective-permute-done | bytes 524320 | tf_op jit(solution)/shard_map/ppermute | solution.py:19
  75.6 54.4 %conditional.7 = (bf16[512,512]{1,0:T(8,128)(2,1)}, bf16[512,8,64]{0,2,1:T(8,128)(2,1)}, bf16[512,8,64]{0,2,1:T(8,128)(2,1)}, bf16[512,8,64]{0,2,1:T(8,128)(2,1)...) conditional(s32[]{:T(128)} %convert_element_type.539, () %tuple.76, (bf16[512,512]{1,0:T(8,128)(2,1)S(1)}, ...), branch_computations={%region_6.7_spmd, %region_7.12_spmd} | conditional | flops 3878450176 | bytes 134601392 | solution.py:295
  107.8 6.5 %fusion.437 = bf16[8,64,512]{2,1,0:T(8,128)(2,1)S(1)} fusion(f32[8,512,522]{1,2,0:T(8,128)} %copy-done.4, f32[8,512]{1,0:T(8,128)S(1)} %fusion.420, f32[8,512]{1,0:T(8,128)S(1)} %get-tuple-element.1338, pred[512,522]{0,1:T(8,128)(4,1)S(1)} %copy-done.32, bf16[512,8,64]{0,2,1:T(8,128)(2,1)} %bitcast.15, bf16[10,8,64]{0,2,1:T(8,128)(2,1)} %copy.131), kind=kOutput, calls=%fused_computation.587 | convolution fusion | flops 285700096 | bytes 9911296 | tf_op jit(solution)/shard_map/cond/branch_1_fun/hqk,khd->qhd/dot_general | solution.py:76
  117.8 10.9 %fusion.432 = f32[512,512]{1,0:T(8,128)S(1)} fusion(bf16[2048,512]{1,0:T(8,128)(2,1)S(1)} %copy-done.71, f32[512,2048]{1,0:T(8,128)} %convolution_add_fusion.4), kind=kOutput, calls=%fused_computation.579 | convolution fusion | flops 1141899264 | bytes 7340032 | tf_op jit(solution)/shard_map/cond/branch_1_fun/dot_general | solution.py:153
  136.1 47.9 %conditional.8 = (bf16[512,512]{1,0:T(8,128)(2,1)}, bf16[512,8,64]{0,2,1:T(8,128)(2,1)}, bf16[512,8,64]{0,2,1:T(8,128)(2,1)}, bf16[512,8,64]{0,2,1:T(8,128)(2,1)...) conditional(s32[]{:T(128)} %convert_element_type.540, () %tuple.78, (bf16[512,512]{1,0:T(8,128)(2,1)S(1)}, ...), branch_computations={%region_12.13_spmd, %region_13.18_spmd} | conditional | flops 3878450176 | bytes 134044168 | solution.py:295
  161.7 6.4 %fusion.521 = bf16[8,64,512]{2,1,0:T(8,128)(2,1)S(1)} fusion(f32[8,512,522]{1,2,0:T(8,128)} %copy-done.5, f32[8,512]{1,0:T(8,128)S(1)} %fusion.504, f32[8,512]{1,0:T(8,128)S(1)} %get-tuple-element.1352, pred[512,522]{0,1:T(8,128)(4,1)S(1)} %concatenate.116, bf16[512,8,64]{0,2,1:T(8,128)(2,1)} %bitcast.28, bf16[10,8,64]{0,2,1:T(8,128)(2,1)S(1)} %copy.133), kind=kOutput, calls=%fused_computation.704 | convolution fusion | flops 285700096 | bytes 9911296 | tf_op jit(solution)/shard_map/cond/branch_1_fun/hqk,khd->qhd/dot_general | solution.py:76
  171.6 10.9 %fusion.516 = f32[512,512]{1,0:T(8,128)S(1)} fusion(bf16[2048,512]{1,0:T(8,128)(2,1)S(1)} %copy-done.72, f32[512,2048]{1,0:T(8,128)} %convolution_add_fusion.7), kind=kOutput, calls=%fused_computation.696 | convolution fusion | flops 1141899264 | bytes 7340032 | tf_op jit(solution)/shard_map/cond/branch_1_fun/dot_general | solution.py:153
  190.0 4.8 select_bitcast_fusion.1
  199.6 75.5 %conditional.9 = (f32[512,512]{0,1:T(8,128)}, f32[10,1024]{1,0:T(8,128)}) conditional(s32[]{:T(128)} %convert_element_type.541, () %tuple.80, (bf16[2,1,512,512]{3,2,1,0:T(8,128)(2,1)}, pred[512,512]{1,0:T(32,128)(4,1)}, bf16[]{:T(256)}, s32[]{:T(128)}, f32[2,512,2048]{2,1,0:T(8,128)}, /*index=5*/bf16[2048,512]{1,0:T(8,128)(2,1)}, ...), branch_computations={%region_18.19_spmd, %region_19.27_spmd} | conditional | flops 4719746048 | bytes 179329520 | solution.py:347
  202.1 6.8 %fusion.63 = f32[8,512,522]{1,2,0:T(8,128)} fusion(bf16[2,512,8,64]{1,3,2,0:T(8,128)(2,1)S(1)} %get-tuple-element.782, s32[]{:T(128)S(6)} %min.25, bf16[512,8,64]{0,2,1:T(8,128)(2,1)} %get-tuple-element.1281, bf16[10,8,64]{0,2,1:T(8,128)(2,1)S(1)} %copy.138), kind=kOutput, calls=%fused_computation.79 | convolution fusion | flops 274747392 | bytes 9732100 | tf_op jit(solution)/shard_map/cond/branch_1_fun/qhd,khd->hqk/dot_general | solution.py:94
  218.0 7.1 %multiply_reduce_fusion = (f32[8,512]{1,0:T(8,128)S(1)}, f32[8,512,522]{1,2,0:T(8,128)S(1)}) fusion(f32[8,512,522]{1,2,0:T(8,128)} %fusion.63, f32[8,512]{1,0:T(8,128)S(1)} %dynamic-slice_bitcast_fusion.2, pred[512,522]{0,1:T(8,128)(4,1)} %concatenate.121, bf16[512,8,64]{0,2,1:T(8,128)(2,1)} %bitcast.622, bf16[512,8,64]{0,2,1:T(8,128)(2,1)} %get-tuple-element.1280, ...), kind=kOutput, calls=%fused_computation.1 | convolution fusion | flops 285433856 | bytes 18463744 | tf_op jit(solution)/shard_map/cond/branch_1_fun/qhd,khd->hqk/dot_general | solution.py:103
  233.3 5.4 %fusion.37 = f32[522,8,64]{0,2,1:T(8,128)S(1)} fusion(bf16[512,8,64]{0,2,1:T(8,128)(2,1)} %bitcast.623, f32[8,512,522]{1,2,0:T(8,128)} %fusion.63, f32[8,512]{1,0:T(8,128)S(1)} %dynamic-slice_bitcast_fusion.2, pred[512,522]{0,1:T(8,128)(4,1)} %concatenate.121), kind=kOutput, calls=%fused_computation.48 | convolution fusion | flops 282230784 | bytes 10429440 | tf_op jit(solution)/shard_map/cond/branch_1_fun/hqk,qhd->khd/dot_general | solution.py:100
  252.8 16.5 %fusion.54 = (f32[512]{0:T(512)S(1)}, f32[512]{0:T(512)S(1)}, f32[512]{0:T(512)S(1)}, f32[512,512]{0,1:T(8,128)}) fusion(f32[512]{0:T(512)S(1)} %broadcast_multiply_fusion, bf16[2,512,512]{1,2,0:T(8,128)(2,1)} %copy.137, s32[]{:T(128)S(6)} %min.25, f32[512,512]{0,1:T(8,128)} %fusion.41, f32[512]{0:T(512)S(1)} %bitcast.681, ...), kind=kOutput, calls=%fused_computation.63 | convolution fusion | flops 2225601024 | bytes 11808256 | tf_op jit(solution)/shard_map/cond/branch_1_fun/dot_general | solution.py:180
  283.3 75.2 %conditional.10 = (f32[512,512]{0,1:T(8,128)}, f32[10,1024]{1,0:T(8,128)}) conditional(s32[]{:T(128)} %convert_element_type.542, () %tuple.82, (pred[512,512]{1,0:T(32,128)(4,1)}, bf16[512,512]{0,1:T(8,128)(2,1)}, bf16[512,512]{0,1:T(8,128)(2,1)}, s32[]{:T(128)}, f32[2,512,2048]{2,1,0:T(8,128)}, /*index=5*/bf16[2048,512]{1,0:T(8,128)(2,1)}, ...), branch_computations={%region_27.28_spmd, %region_28.36_spmd} | conditional | flops 4719221760 | bytes 178427408 | solution.py:347
  286.5 6.8 %fusion.179 = f32[8,512,522]{1,2,0:T(8,128)} fusion(bf16[2,512,8,64]{1,3,2,0:T(8,128)(2,1)S(1)} %get-tuple-element.801, s32[]{:T(128)S(6)} %min.26, bf16[512,8,64]{0,2,1:T(8,128)(2,1)} %get-tuple-element.1297, bf16[10,8,64]{0,2,1:T(8,128)(2,1)S(1)} %copy.143), kind=kOutput, calls=%fused_computation.224 | convolution fusion | flops 274747392 | bytes 9732100 | tf_op jit(solution)/shard_map/cond/branch_1_fun/qhd,khd->hqk/dot_general | solution.py:94
  301.2 7.1 %multiply_reduce_fusion.1 = (f32[8,512]{1,0:T(8,128)S(1)}, f32[8,512,522]{1,2,0:T(8,128)S(1)}) fusion(f32[8,512,522]{1,2,0:T(8,128)} %fusion.179, f32[8,512]{1,0:T(8,128)S(1)} %dynamic-slice_bitcast_fusion.5, pred[512,522]{0,1:T(8,128)(4,1)} %concatenate.126, bf16[512,8,64]{0,2,1:T(8,128)(2,1)} %bitcast.615, bf16[512,8,64]{0,2,1:T(8,128)(2,1)} %get-tuple-element.1296, ...), kind=kOutput, calls=%fused_computation.148 | convolution fusion | flops 285433856 | bytes 18463744 | tf_op jit(solution)/shard_map/cond/branch_1_fun/qhd,khd->hqk/dot_general | solution.py:103
  316.7 5.5 %fusion.154 = f32[522,8,64]{0,2,1:T(8,128)S(1)} fusion(bf16[512,8,64]{0,2,1:T(8,128)(2,1)} %bitcast.616, f32[8,512,522]{1,2,0:T(8,128)} %fusion.179, f32[8,512]{1,0:T(8,128)S(1)} %dynamic-slice_bitcast_fusion.5, pred[512,522]{0,1:T(8,128)(4,1)} %concatenate.126), kind=kOutput, calls=%fused_computation.195 | convolution fusion | flops 282230784 | bytes 10429440 | tf_op jit(solution)/shard_map/cond/branch_1_fun/hqk,qhd->khd/dot_general | solution.py:100
  336.1 16.5 %fusion.171 = (f32[512]{0:T(512)S(1)}, f32[512]{0:T(512)S(1)}, f32[512]{0:T(512)S(1)}, f32[512,512]{0,1:T(8,128)}) fusion(f32[512]{0:T(512)S(1)} %broadcast_multiply_fusion.1, bf16[2,512,512]{1,2,0:T(8,128)(2,1)} %copy.142, s32[]{:T(128)S(6)} %min.26, f32[512,512]{0,1:T(8,128)} %fusion.158, f32[512]{0:T(512)S(1)} %bitcast.682, ...), kind=kOutput, calls=%fused_computation.210 | convolution fusion | flops 2225338880 | bytes 11545600 | tf_op jit(solution)/shard_map/cond/branch_1_fun/dot_general | solution.py:180
  370.2 4.6 conditional.11
  379.8 75.0 %reduce-scatter.2.cloned.1.call-done = f32[10,256]{1,0:T(8,128)} async-done(((f32[10,1024]{1,0:T(8,128)}), f32[10,256]{1,0:T(8,128)}) %reduce-scatter.2.cloned.1.call-update) | async-done | bytes 10256 | tf_op jit(solution)/shard_map/reduce_scatter | solution.py:362
  454.7 15.6 %psum.14 = f32[10,256]{1,0:T(8,128)S(1)} all-reduce(f32[10,256]{1,0:T(8,128)} %reduce-scatter.2.cloned.1.call-done), channel_id=1, replica_groups=mesh['pipe'=2,'grp'=4,'dp'=4] {'grp'}, use_global_device_ids=true, to_apply=%region_46.47 | all-reduce | flops 2560 | bytes 20480 | tf_op jit(solution)/shard_map/psum | solution.py:363
  473.3 31.4 %psum.15 = f32[10,512]{1,0:T(8,128)S(1)} all-reduce(f32[10,512]{1,0:T(8,128)S(1)} %fusion.588), channel_id=1, replica_groups=mesh['pipe'=2,'grp'=4,'dp'=4] {'pipe','dp'}, use_global_device_ids=true, to_apply=%region_47.48 | all-reduce | flops 5120 | bytes 40960 | tf_op jit(solution)/shard_map/psum | solution.py:370
  (339 shorter events, 209.9 us)
Async XLA Ops:
  7.2 8.9 %copy-start.15 = (bf16[2,1,512,512]{3,2,1,0:T(8,128)(2,1)S(1)}, bf16[2,1,512,512]{3,2,1,0:T(8,128)(2,1)}, u32[]{:S(2)}) copy-start(bf16[2,1,512,512]{3,2,1,0:T(8,128)(2,1)} %param.32) | copy-start | bytes 3145732
  7.2 8.9 %copy-start.22 = (bf16[1,512,512]{2,1,0:T(8,128)(2,1)S(1)}, bf16[1,512,512]{2,1,0:T(8,128)(2,1)}, u32[]{:S(2)}) copy-start(bf16[1,512,512]{2,1,0:T(8,128)(2,1)} %param.39) | copy-start | bytes 1572868
  7.2 8.9 %copy-start.53 = (s32[2,1,512]{2,1,0:T(1,128)S(1)}, s32[2,1,512]{2,1,0:T(1,128)}, u32[]{:S(2)}) copy-start(s32[2,1,512]{2,1,0:T(1,128)} %param.34) | copy-start | bytes 12292
  7.2 8.9 %copy-start.89 = (f32[1,512]{1,0:T(1,128)S(1)}, f32[1,512]{1,0:T(1,128)}, u32[]{:S(2)}) copy-start(f32[1,512]{1,0:T(1,128)} %param.35) | copy-start | bytes 6148
  7.2 8.9 %copy-start.79 = (f32[1,512]{1,0:T(1,128)S(1)}, f32[1,512]{1,0:T(1,128)}, u32[]{:S(2)}) copy-start(f32[1,512]{1,0:T(1,128)} %param.36) | copy-start | bytes 6148
  7.2 8.9 %copy-start.52 = (f32[1,1536]{1,0:T(1,128)S(1)}, f32[1,1536]{1,0:T(1,128)}, u32[]{:S(2)}) copy-start(f32[1,1536]{1,0:T(1,128)} %param.38) | copy-start | bytes 18436
  7.3 447.5 %reduce-scatter.2.cloned.1.call-start = ((), (), s32[]{:S(2)}) async-start(), calls=%async_computation.1 | async-start | bytes 81920 | tf_op jit(solution)/shard_map/reduce_scatter | solution.py:362
  30.6 43.1 %collective-permute-start = (bf16[512,512]{1,0:T(8,128)(2,1)}, bf16[512,512]{1,0:T(8,128)(2,1)}, u32[]{:S(2)}, u32[]{:S(2)}) collective-permute-start(bf16[512,512]{1,0:T(8,128)(2,1)} %get-tuple-element.858), channel_id=1, source_target_pairs={{0,16},{1,17},{2,18},{3,19},{4,20},{5,21},{6,22},{7,23},{8,24},{9,... | collective-permute-start | bytes 1572872 | tf_op jit(solution)/shard_map/ppermute | solution.py:19
  82.5 10.0 %copy-start.56 = (s32[2,1,512]{2,1,0:T(1,128)S(1)}, s32[2,1,512]{2,1,0:T(1,128)}, u32[]{:S(2)}) copy-start(s32[2,1,512]{2,1,0:T(1,128)} %get-tuple-element.742) | copy-start | bytes 12292 | tf_op jit(solution)/shard_map/cond
  98.8 8.9 %copy-start.32 = (pred[512,522]{0,1:T(8,128)(4,1)S(1)}, pred[512,522]{0,1:T(8,128)(4,1)}, u32[]{:S(2)}) copy-start(pred[512,522]{0,1:T(8,128)(4,1)} %concatenate.111) | copy-start | bytes 801796 | tf_op jit(solution)/shard_map/cond
  117.8 10.9 %copy-start.81 = (f32[1,512]{1,0:T(1,128)S(1)}, f32[1,512]{1,0:T(1,128)}, u32[]{:S(2)}) copy-start(f32[1,512]{1,0:T(1,128)} %get-tuple-element.746) | copy-start | bytes 6148 | tf_op jit(solution)/shard_map/cond
  117.8 10.9 %copy-start.87 = (f32[1,512]{1,0:T(1,128)S(1)}, f32[1,512]{1,0:T(1,128)}, u32[]{:S(2)}) copy-start(f32[1,512]{1,0:T(1,128)} %get-tuple-element.752) | copy-start | bytes 6148 | tf_op jit(solution)/shard_map/cond
  130.0 4.1 collective-permute-start.1
  143.0 8.7 %copy-start.57 = (s32[2,1,512]{2,1,0:T(1,128)S(1)}, s32[2,1,512]{2,1,0:T(1,128)}, u32[]{:S(2)}) copy-start(s32[2,1,512]{2,1,0:T(1,128)} %get-tuple-element.759) | copy-start | bytes 12292 | tf_op jit(solution)/shard_map/cond
  171.6 10.9 %copy-start.23 = (bf16[512,512]{1,0:T(8,128)(2,1)S(1)}, bf16[512,512]{1,0:T(8,128)(2,1)}, u32[]{:S(2)}) copy-start(bf16[512,512]{1,0:T(8,128)(2,1)} %get-tuple-element.762) | copy-start | bytes 1572868 | tf_op jit(solution)/shard_map/cond
  171.6 10.9 %copy-start.82 = (f32[1,512]{1,0:T(1,128)S(1)}, f32[1,512]{1,0:T(1,128)}, u32[]{:S(2)}) copy-start(f32[1,512]{1,0:T(1,128)} %get-tuple-element.763) | copy-start | bytes 6148 | tf_op jit(solution)/shard_map/cond
  171.6 10.9 %copy-start.88 = (f32[1,512]{1,0:T(1,128)S(1)}, f32[1,512]{1,0:T(1,128)}, u32[]{:S(2)}) copy-start(f32[1,512]{1,0:T(1,128)} %get-tuple-element.769) | copy-start | bytes 6148 | tf_op jit(solution)/shard_map/cond
  187.5 12.1 %copy-start.48 = (f32[2,8,512]{2,1,0:T(8,128)}, f32[2,8,512]{2,1,0:T(8,128)S(1)}, u32[]{:S(2)}) copy-start(f32[2,8,512]{2,1,0:T(8,128)S(1)} %pad_maximum_fusion.23) | copy-start | bytes 98308
  216.4 8.7 %slice-start.6 = ((s8[8650752]{0:T(1024)(128)(4,1)}), s8[262144]{0:T(1024)(128)(4,1)S(1)}, s32[]{:S(2)}) async-start(s8[8650752]{0:T(1024)(128)(4,1)} %bitcast.590), calls=%async_computation.8 | async-start | bytes 524288 | tf_op jit(solution)/shard_map/cond
  277.2 6.1 %collective-permute-start.2 = (bf16[512,512]{0,1:T(8,128)(2,1)}, bf16[512,512]{0,1:T(8,128)(2,1)}, u32[]{:S(2)}, u32[]{:S(2)}) collective-permute-start(bf16[512,512]{0,1:T(8,128)(2,1)} %convert_element_type.543), channel_id=1, source_target_pairs={{16,0},{17,1},{18,2},{19,3},{20,4},{21,5},{22,6},{23,7},{24,8},{25... | collective-permute-start | bytes 1572872 | tf_op jit(solution)/shard_map/ppermute | solution.py:19
  299.6 8.7 %slice-start.3 = ((s8[8650752]{0:T(1024)(128)(4,1)}), s8[262144]{0:T(1024)(128)(4,1)S(1)}, s32[]{:S(2)}) async-start(s8[8650752]{0:T(1024)(128)(4,1)} %bitcast.588), calls=%async_computation.5 | async-start | bytes 524288 | tf_op jit(solution)/shard_map/cond
  360.6 9.6 %collective-permute-start.3 = (bf16[512,512]{0,1:T(8,128)(2,1)}, bf16[512,512]{0,1:T(8,128)(2,1)}, u32[]{:S(2)}, u32[]{:S(2)}) collective-permute-start(bf16[512,512]{0,1:T(8,128)(2,1)} %convert_element_type.545), channel_id=1, source_target_pairs={{16,0},{17,1},{18,2},{19,3},{20,4},{21,5},{22,6},{23,7},{24,8},{25... | collective-permute-start | bytes 1572872 | tf_op jit(solution)/shard_map/ppermute | solution.py:19
  376.3 94.0 %copy-start.28 = (f32[10,512]{1,0:T(8,128)S(1)}, f32[10,512]{1,0:T(8,128)}, u32[]{:S(2)}) copy-start(f32[10,512]{1,0:T(8,128)} %copy-done.27) | copy-start | bytes 61444
  376.3 128.4 %copy-start.51 = (f32[10,512]{1,0:T(8,128)S(1)}, f32[10,512]{1,0:T(8,128)}, u32[]{:S(2)}) copy-start(f32[10,512]{1,0:T(8,128)} %param.47) | copy-start | bytes 61444
  (59 other events, 274.2 us)
Sparse Core Ops, SparseCore 0:
  376.5 78.2 reduce-scatter.1
where the time goes:
time: 522 us; the launch traced here: 517 us
  matrix products  158 us (30%)
  waiting for transfers between devices  120 us (23%)
  local copies, waits for them, and re-layouts  89.4 us (17%)
  other arithmetic  68.3 us (13%)
  blocking collectives  47 us (9%)
  between operations  14.6 us (3%)
  loops' own time  13.2 us (3%)
  starting transfers between devices  6.84 us (1%)
    reduce_scatter x1, waiting for transfers between devices, local(): lax.psum_scatter(prefix_total, 'dp', scatter_dimension=1, tiled=True)  75 us
    ppermute x4, waiting for transfers between devices, passed_along(): return lax.ppermute(shard, axis, pairs)  44.6 us
    dot_general x2, matrix products, backward_layer(): jnp.dot(grad_before, w_in.T, preferred_element_type=jnp.float32)  33 us
    psum x1, blocking collectives, local(): hidden_grad = lax.psum(hidden_part, ('pipe', 'dp'))  31.4 us
    another operation x21, local copies, waits for them, and re-layouts  22.9 us
    dot_general x2, matrix products, forward_layer(): jnp.dot(activated, w_back, preferred_element_type=jnp.float32)  21.8 us
    psum x1, blocking collectives, local(): local_cols = lax.psum(local_cols, 'grp')  15.6 us
    cond x118, local copies, waits for them, and re-layouts  15.1 us
  transfers between devices with their start and end apart: 5, of which 3 were waited for; matrix products, arithmetic and copies ran while one was open for 3% of the time, Pallas kernels for 0%

commit v1 on v0

--- a/solution.py
+++ b/solution.py
@@ -360,7 +360,19 @@
     dp_index = lax.axis_index("dp")
     col_width = 2 * D // lax.axis_size("dp")
     local_cols = lax.psum_scatter(prefix_total, "dp", scatter_dimension=1, tiled=True)
-    local_cols = lax.psum(local_cols, "grp")
+
+    def _solve_ports(slab_in):
+        mesh_dim = "grp"
+        axis_len = lax.axis_size(mesh_dim)
+        piece_next = lambda local_part: [(nth, nth ^ local_part) for nth in range(axis_len)]
+        spare = slab_in
+        for num in range(axis_len.bit_length() - 1):
+            u_next = piece_next(1 << num)
+            x_new = lax.ppermute(spare, axis_name=mesh_dim, perm=u_next)
+            spare = spare + x_new
+        return spare
+
+    local_cols = _solve_ports(local_cols)
     grad_out_weight = matmul_hi(hidden_units.T, local_cols)
     grad_out_bias = jnp.sum(local_cols, axis=0)
     out_cols = lax.dynamic_slice_in_dim(

time: 522 us -> 509 us (0.975)
  blocking collectives: 47 us -> 29.9 us
    psum x1 -> x0, blocking collectives: 15.6 us -> none  [local(): local_cols = lax.psum(local_cols, 'grp')]
  transfers between devices with their start and end apart: 5 -> 7, of which waited for: 3 -> 4; matrix products, arithmetic and copies ran while one was open for 3% -> 3% of each run, Pallas kernels for 0% -> 0%
where the time goes in v1:
time: 509 us; the launch traced here: 503 us
  matrix products  158 us (31%)
  waiting for transfers between devices  120 us (24%)
  local copies, waits for them, and re-layouts  87.9 us (17%)
  other arithmetic  69.1 us (14%)
  blocking collectives  29.9 us (6%)
  between operations  14.6 us (3%)
  loops' own time  13.5 us (3%)
  starting transfers between devices  10.1 us (2%)
    reduce_scatter x1, waiting for transfers between devices, local(): lax.psum_scatter(prefix_total, 'dp', scatter_dimension=1, tiled=True)  74.4 us
    ppermute x4, waiting for transfers between devices, passed_along(): return lax.ppermute(shard, axis, pairs)  44.6 us
    dot_general x2, matrix products, backward_layer(): jnp.dot(grad_before, w_in.T, preferred_element_type=jnp.float32)  33 us
    psum x1, blocking collectives, local(): hidden_grad = lax.psum(hidden_part, ('pipe', 'dp'))  29.9 us
    another operation x21, local copies, waits for them, and re-layouts  22.7 us
    dot_general x2, matrix products, forward_layer(): jnp.dot(activated, w_back, preferred_element_type=jnp.float32)  21.8 us
    cond x118, local copies, waits for them, and re-layouts  15 us
    another operation x9, other arithmetic, local(): jnp.stack(leaf_list)  14.7 us
  transfers between devices with their start and end apart: 7, of which 4 were waited for; matrix products, arithmetic and copies ran while one was open for 3% of the time, Pallas kernels for 0%

profile of v1, /device:TPU:1, one launch (start us, length us, event | category | flops | bytes accessed | tf_op | source)
XLA Modules:
  0.0 503.4 jit_solution(17883562240558342991)
XLA Ops:
  10.4 4.3 fusion.607
  16.2 14.3 %conditional.6 = (bf16[512,512]{1,0:T(8,128)(2,1)}, bf16[512,8,64]{0,2,1:T(8,128)(2,1)}, bf16[512,8,64]{0,2,1:T(8,128)(2,1)}, bf16[512,8,64]{0,2,1:T(8,128)(2,1)...) conditional(s32[]{:T(128)} %convert_element_type.537, () %tuple.74, (bf16[512,512]{1,0:T(8,128)(2,1)S(1)}, ...), branch_computations={%region_0.1_spmd, %region_1.6_spmd} | conditional | flops 3878450176 | bytes 134584976 | solution.py:295
  31.8 41.8 %collective-permute-done = bf16[512,512]{1,0:T(8,128)(2,1)} collective-permute-done((bf16[512,512]{1,0:T(8,128)(2,1)}, bf16[512,512]{1,0:T(8,128)(2,1)}, u32[]{:S(2)}, u32[]{:S(2)}) %collective-permute-start) | collective-permute-done | bytes 524320 | tf_op jit(solution)/shard_map/ppermute | solution.py:19
  75.5 54.5 %conditional.7 = (bf16[512,512]{1,0:T(8,128)(2,1)}, bf16[512,8,64]{0,2,1:T(8,128)(2,1)}, bf16[512,8,64]{0,2,1:T(8,128)(2,1)}, bf16[512,8,64]{0,2,1:T(8,128)(2,1)...) conditional(s32[]{:T(128)} %convert_element_type.539, () %tuple.76, (bf16[512,512]{1,0:T(8,128)(2,1)S(1)}, ...), branch_computations={%region_6.7_spmd, %region_7.12_spmd} | conditional | flops 3878450176 | bytes 134601392 | solution.py:295
  107.7 6.5 %fusion.437 = bf16[8,64,512]{2,1,0:T(8,128)(2,1)S(1)} fusion(f32[8,512,522]{1,2,0:T(8,128)} %copy-done.4, f32[8,512]{1,0:T(8,128)S(1)} %fusion.420, f32[8,512]{1,0:T(8,128)S(1)} %get-tuple-element.1338, pred[512,522]{0,1:T(8,128)(4,1)S(1)} %copy-done.33, bf16[512,8,64]{0,2,1:T(8,128)(2,1)} %bitcast.15, bf16[10,8,64]{0,2,1:T(8,128)(2,1)} %copy.131), kind=kOutput, calls=%fused_computation.587 | convolution fusion | flops 285700096 | bytes 9911296 | tf_op jit(solution)/shard_map/cond/branch_1_fun/hqk,khd->qhd/dot_general | solution.py:76
  117.7 10.9 %fusion.432 = f32[512,512]{1,0:T(8,128)S(1)} fusion(bf16[2048,512]{1,0:T(8,128)(2,1)S(1)} %copy-done.73, f32[512,2048]{1,0:T(8,128)} %convolution_add_fusion.4), kind=kOutput, calls=%fused_computation.579 | convolution fusion | flops 1141899264 | bytes 7340032 | tf_op jit(solution)/shard_map/cond/branch_1_fun/dot_general | solution.py:153
  136.1 47.8 %conditional.8 = (bf16[512,512]{1,0:T(8,128)(2,1)}, bf16[512,8,64]{0,2,1:T(8,128)(2,1)}, bf16[512,8,64]{0,2,1:T(8,128)(2,1)}, bf16[512,8,64]{0,2,1:T(8,128)(2,1)...) conditional(s32[]{:T(128)} %convert_element_type.540, () %tuple.78, (bf16[512,512]{1,0:T(8,128)(2,1)S(1)}, ...), branch_computations={%region_12.13_spmd, %region_13.18_spmd} | conditional | flops 3878450176 | bytes 134044168 | solution.py:295
  161.7 6.4 %fusion.521 = bf16[8,64,512]{2,1,0:T(8,128)(2,1)S(1)} fusion(f32[8,512,522]{1,2,0:T(8,128)} %copy-done.5, f32[8,512]{1,0:T(8,128)S(1)} %fusion.504, f32[8,512]{1,0:T(8,128)S(1)} %get-tuple-element.1352, pred[512,522]{0,1:T(8,128)(4,1)S(1)} %concatenate.116, bf16[512,8,64]{0,2,1:T(8,128)(2,1)} %bitcast.28, bf16[10,8,64]{0,2,1:T(8,128)(2,1)S(1)} %copy.133), kind=kOutput, calls=%fused_computation.704 | convolution fusion | flops 285700096 | bytes 9911296 | tf_op jit(solution)/shard_map/cond/branch_1_fun/hqk,khd->qhd/dot_general | solution.py:76
  171.5 10.9 %fusion.516 = f32[512,512]{1,0:T(8,128)S(1)} fusion(bf16[2048,512]{1,0:T(8,128)(2,1)S(1)} %copy-done.74, f32[512,2048]{1,0:T(8,128)} %convolution_add_fusion.7), kind=kOutput, calls=%fused_computation.696 | convolution fusion | flops 1141899264 | bytes 7340032 | tf_op jit(solution)/shard_map/cond/branch_1_fun/dot_general | solution.py:153
  189.9 4.8 select_bitcast_fusion.1
  194.7 3.9 pad_maximum_fusion.18
  199.5 75.5 %conditional.9 = (f32[512,512]{0,1:T(8,128)}, f32[10,1024]{1,0:T(8,128)}) conditional(s32[]{:T(128)} %convert_element_type.541, () %tuple.80, (bf16[2,1,512,512]{3,2,1,0:T(8,128)(2,1)}, pred[512,512]{1,0:T(32,128)(4,1)}, bf16[]{:T(256)}, s32[]{:T(128)}, f32[2,512,2048]{2,1,0:T(8,128)}, /*index=5*/bf16[2048,512]{1,0:T(8,128)(2,1)}, ...), branch_computations={%region_18.19_spmd, %region_19.27_spmd} | conditional | flops 4719746048 | bytes 179329520 | solution.py:347
  202.0 6.8 %fusion.63 = f32[8,512,522]{1,2,0:T(8,128)} fusion(bf16[2,512,8,64]{1,3,2,0:T(8,128)(2,1)S(1)} %get-tuple-element.782, s32[]{:T(128)S(6)} %min.25, bf16[512,8,64]{0,2,1:T(8,128)(2,1)} %get-tuple-element.1281, bf16[10,8,64]{0,2,1:T(8,128)(2,1)S(1)} %copy.138), kind=kOutput, calls=%fused_computation.79 | convolution fusion | flops 274747392 | bytes 9732100 | tf_op jit(solution)/shard_map/cond/branch_1_fun/qhd,khd->hqk/dot_general | solution.py:94
  217.9 7.1 %multiply_reduce_fusion = (f32[8,512]{1,0:T(8,128)S(1)}, f32[8,512,522]{1,2,0:T(8,128)S(1)}) fusion(f32[8,512,522]{1,2,0:T(8,128)} %fusion.63, f32[8,512]{1,0:T(8,128)S(1)} %dynamic-slice_bitcast_fusion.2, pred[512,522]{0,1:T(8,128)(4,1)} %concatenate.121, bf16[512,8,64]{0,2,1:T(8,128)(2,1)} %bitcast.620, bf16[512,8,64]{0,2,1:T(8,128)(2,1)} %get-tuple-element.1280, ...), kind=kOutput, calls=%fused_computation.1 | convolution fusion | flops 285433856 | bytes 18463744 | tf_op jit(solution)/shard_map/cond/branch_1_fun/qhd,khd->hqk/dot_general | solution.py:103
  233.1 5.4 %fusion.37 = f32[522,8,64]{0,2,1:T(8,128)S(1)} fusion(bf16[512,8,64]{0,2,1:T(8,128)(2,1)} %bitcast.621, f32[8,512,522]{1,2,0:T(8,128)} %fusion.63, f32[8,512]{1,0:T(8,128)S(1)} %dynamic-slice_bitcast_fusion.2, pred[512,522]{0,1:T(8,128)(4,1)} %concatenate.121), kind=kOutput, calls=%fused_computation.48 | convolution fusion | flops 282230784 | bytes 10429440 | tf_op jit(solution)/shard_map/cond/branch_1_fun/hqk,qhd->khd/dot_general | solution.py:100
  252.7 16.5 %fusion.54 = (f32[512]{0:T(512)S(1)}, f32[512]{0:T(512)S(1)}, f32[512]{0:T(512)S(1)}, f32[512,512]{0,1:T(8,128)}) fusion(f32[512]{0:T(512)S(1)} %broadcast_multiply_fusion, bf16[2,512,512]{1,2,0:T(8,128)(2,1)} %copy.137, s32[]{:T(128)S(6)} %min.25, f32[512,512]{0,1:T(8,128)} %fusion.41, f32[512]{0:T(512)S(1)} %bitcast.679, ...), kind=kOutput, calls=%fused_computation.63 | convolution fusion | flops 2225601024 | bytes 11808256 | tf_op jit(solution)/shard_map/cond/branch_1_fun/dot_general | solution.py:180
  283.1 75.1 %conditional.10 = (f32[512,512]{0,1:T(8,128)}, f32[10,1024]{1,0:T(8,128)}) conditional(s32[]{:T(128)} %convert_element_type.542, () %tuple.82, (pred[512,512]{1,0:T(32,128)(4,1)}, bf16[512,512]{0,1:T(8,128)(2,1)}, bf16[512,512]{0,1:T(8,128)(2,1)}, s32[]{:T(128)}, f32[2,512,2048]{2,1,0:T(8,128)}, /*index=5*/bf16[2048,512]{1,0:T(8,128)(2,1)}, ...), branch_computations={%region_27.28_spmd, %region_28.36_spmd} | conditional | flops 4719221760 | bytes 178427408 | solution.py:347
  286.3 6.8 %fusion.179 = f32[8,512,522]{1,2,0:T(8,128)} fusion(bf16[2,512,8,64]{1,3,2,0:T(8,128)(2,1)S(1)} %get-tuple-element.801, s32[]{:T(128)S(6)} %min.26, bf16[512,8,64]{0,2,1:T(8,128)(2,1)} %get-tuple-element.1297, bf16[10,8,64]{0,2,1:T(8,128)(2,1)S(1)} %copy.143), kind=kOutput, calls=%fused_computation.224 | convolution fusion | flops 274747392 | bytes 9732100 | tf_op jit(solution)/shard_map/cond/branch_1_fun/qhd,khd->hqk/dot_general | solution.py:94
  301.0 7.1 %multiply_reduce_fusion.1 = (f32[8,512]{1,0:T(8,128)S(1)}, f32[8,512,522]{1,2,0:T(8,128)S(1)}) fusion(f32[8,512,522]{1,2,0:T(8,128)} %fusion.179, f32[8,512]{1,0:T(8,128)S(1)} %dynamic-slice_bitcast_fusion.5, pred[512,522]{0,1:T(8,128)(4,1)} %concatenate.126, bf16[512,8,64]{0,2,1:T(8,128)(2,1)} %bitcast.613, bf16[512,8,64]{0,2,1:T(8,128)(2,1)} %get-tuple-element.1296, ...), kind=kOutput, calls=%fused_computation.148 | convolution fusion | flops 285433856 | bytes 18463744 | tf_op jit(solution)/shard_map/cond/branch_1_fun/qhd,khd->hqk/dot_general | solution.py:103
  316.4 5.4 %fusion.154 = f32[522,8,64]{0,2,1:T(8,128)S(1)} fusion(bf16[512,8,64]{0,2,1:T(8,128)(2,1)} %bitcast.614, f32[8,512,522]{1,2,0:T(8,128)} %fusion.179, f32[8,512]{1,0:T(8,128)S(1)} %dynamic-slice_bitcast_fusion.5, pred[512,522]{0,1:T(8,128)(4,1)} %concatenate.126), kind=kOutput, calls=%fused_computation.195 | convolution fusion | flops 282230784 | bytes 10429440 | tf_op jit(solution)/shard_map/cond/branch_1_fun/hqk,qhd->khd/dot_general | solution.py:100
  335.8 16.5 %fusion.171 = (f32[512]{0:T(512)S(1)}, f32[512]{0:T(512)S(1)}, f32[512]{0:T(512)S(1)}, f32[512,512]{0,1:T(8,128)}) fusion(f32[512]{0:T(512)S(1)} %broadcast_multiply_fusion.1, bf16[2,512,512]{1,2,0:T(8,128)(2,1)} %copy.142, s32[]{:T(128)S(6)} %min.26, f32[512,512]{0,1:T(8,128)} %fusion.158, f32[512]{0:T(512)S(1)} %bitcast.680, ...), kind=kOutput, calls=%fused_computation.210 | convolution fusion | flops 2225338880 | bytes 11545600 | tf_op jit(solution)/shard_map/cond/branch_1_fun/dot_general | solution.py:180
  367.2 4.8 conditional.11
  377.5 74.4 %reduce-scatter.2.cloned.1.call-done = f32[10,256]{1,0:T(8,128)} async-done(((f32[10,1024]{1,0:T(8,128)}), f32[10,256]{1,0:T(8,128)}) %reduce-scatter.2.cloned.1.call-update) | async-done | bytes 10256 | tf_op jit(solution)/shard_map/reduce_scatter | solution.py:362
  459.9 29.9 %psum.7 = f32[10,512]{1,0:T(8,128)S(1)} all-reduce(f32[10,512]{1,0:T(8,128)S(1)} %fusion.588), channel_id=1, replica_groups=mesh['pipe'=2,'grp'=4,'dp'=4] {'pipe','dp'}, use_global_device_ids=true, to_apply=%region_46.47 | all-reduce | flops 5120 | bytes 40960 | tf_op jit(solution)/shard_map/psum | solution.py:382
  (347 shorter events, 209.9 us)
Async XLA Ops:
  7.2 8.9 %copy-start.23 = (bf16[1,512,512]{2,1,0:T(8,128)(2,1)S(1)}, bf16[1,512,512]{2,1,0:T(8,128)(2,1)}, u32[]{:S(2)}) copy-start(bf16[1,512,512]{2,1,0:T(8,128)(2,1)} %param.39) | copy-start | bytes 1572868
  7.2 8.9 %copy-start.54 = (s32[2,1,512]{2,1,0:T(1,128)S(1)}, s32[2,1,512]{2,1,0:T(1,128)}, u32[]{:S(2)}) copy-start(s32[2,1,512]{2,1,0:T(1,128)} %param.34) | copy-start | bytes 12292
  7.2 8.9 %copy-start.91 = (f32[1,512]{1,0:T(1,128)S(1)}, f32[1,512]{1,0:T(1,128)}, u32[]{:S(2)}) copy-start(f32[1,512]{1,0:T(1,128)} %param.35) | copy-start | bytes 6148
  7.3 444.6 %reduce-scatter.2.cloned.1.call-start = ((), (), s32[]{:S(2)}) async-start(), calls=%async_computation.1 | async-start | bytes 81920 | tf_op jit(solution)/shard_map/reduce_scatter | solution.py:362
  30.5 43.1 %collective-permute-start = (bf16[512,512]{1,0:T(8,128)(2,1)}, bf16[512,512]{1,0:T(8,128)(2,1)}, u32[]{:S(2)}, u32[]{:S(2)}) collective-permute-start(bf16[512,512]{1,0:T(8,128)(2,1)} %get-tuple-element.858), channel_id=1, source_target_pairs={{0,16},{1,17},{2,18},{3,19},{4,20},{5,21},{6,22},{7,23},{8,24},{9,... | collective-permute-start | bytes 1572872 | tf_op jit(solution)/shard_map/ppermute | solution.py:19
  82.4 9.9 %copy-start.57 = (s32[2,1,512]{2,1,0:T(1,128)S(1)}, s32[2,1,512]{2,1,0:T(1,128)}, u32[]{:S(2)}) copy-start(s32[2,1,512]{2,1,0:T(1,128)} %get-tuple-element.742) | copy-start | bytes 12292 | tf_op jit(solution)/shard_map/cond
  98.7 9.0 %copy-start.33 = (pred[512,522]{0,1:T(8,128)(4,1)S(1)}, pred[512,522]{0,1:T(8,128)(4,1)}, u32[]{:S(2)}) copy-start(pred[512,522]{0,1:T(8,128)(4,1)} %concatenate.111) | copy-start | bytes 801796 | tf_op jit(solution)/shard_map/cond
  117.7 10.9 %copy-start.83 = (f32[1,512]{1,0:T(1,128)S(1)}, f32[1,512]{1,0:T(1,128)}, u32[]{:S(2)}) copy-start(f32[1,512]{1,0:T(1,128)} %get-tuple-element.746) | copy-start | bytes 6148 | tf_op jit(solution)/shard_map/cond
  117.7 10.9 %copy-start.89 = (f32[1,512]{1,0:T(1,128)S(1)}, f32[1,512]{1,0:T(1,128)}, u32[]{:S(2)}) copy-start(f32[1,512]{1,0:T(1,128)} %get-tuple-element.752) | copy-start | bytes 6148 | tf_op jit(solution)/shard_map/cond
  130.0 4.1 collective-permute-start.1
  171.5 10.9 %copy-start.24 = (bf16[512,512]{1,0:T(8,128)(2,1)S(1)}, bf16[512,512]{1,0:T(8,128)(2,1)}, u32[]{:S(2)}) copy-start(bf16[512,512]{1,0:T(8,128)(2,1)} %get-tuple-element.762) | copy-start | bytes 1572868 | tf_op jit(solution)/shard_map/cond
  171.5 10.9 %copy-start.84 = (f32[1,512]{1,0:T(1,128)S(1)}, f32[1,512]{1,0:T(1,128)}, u32[]{:S(2)}) copy-start(f32[1,512]{1,0:T(1,128)} %get-tuple-element.763) | copy-start | bytes 6148 | tf_op jit(solution)/shard_map/cond
  171.5 10.9 %copy-start.90 = (f32[1,512]{1,0:T(1,128)S(1)}, f32[1,512]{1,0:T(1,128)}, u32[]{:S(2)}) copy-start(f32[1,512]{1,0:T(1,128)} %get-tuple-element.769) | copy-start | bytes 6148 | tf_op jit(solution)/shard_map/cond
  187.4 12.1 %copy-start.49 = (f32[2,8,512]{2,1,0:T(8,128)}, f32[2,8,512]{2,1,0:T(8,128)S(1)}, u32[]{:S(2)}) copy-start(f32[2,8,512]{2,1,0:T(8,128)S(1)} %pad_maximum_fusion.23) | copy-start | bytes 98308
  277.1 6.0 %collective-permute-start.2 = (bf16[512,512]{0,1:T(8,128)(2,1)}, bf16[512,512]{0,1:T(8,128)(2,1)}, u32[]{:S(2)}, u32[]{:S(2)}) collective-permute-start(bf16[512,512]{0,1:T(8,128)(2,1)} %convert_element_type.543), channel_id=1, source_target_pairs={{16,0},{17,1},{18,2},{19,3},{20,4},{21,5},{22,6},{23,7},{24,8},{25... | collective-permute-start | bytes 1572872 | tf_op jit(solution)/shard_map/ppermute | solution.py:19
  358.2 9.0 %copy-start.41 = (bf16[10,8,64]{2,1,0:T(8,128)(2,1)S(1)}, bf16[10,8,64]{2,1,0:T(8,128)(2,1)}, u32[]{:S(2)}) copy-start(bf16[10,8,64]{2,1,0:T(8,128)(2,1)} %reshape.734) | copy-start | bytes 30724
  358.2 9.0 %copy-start.50 = (f32[2,8,512]{2,1,0:T(8,128)S(1)}, f32[2,8,512]{2,1,0:T(8,128)}, u32[]{:S(2)}) copy-start(f32[2,8,512]{2,1,0:T(8,128)} %copy-done.49) | copy-start | bytes 98308
  358.2 9.0 %copy-start.56 = (s32[2,1,512]{2,1,0:T(1,128)S(1)}, s32[2,1,512]{2,1,0:T(1,128)}, u32[]{:S(2)}) copy-start(s32[2,1,512]{2,1,0:T(1,128)} %param.34) | copy-start | bytes 12292
  360.4 6.8 %collective-permute-start.3 = (bf16[512,512]{0,1:T(8,128)(2,1)}, bf16[512,512]{0,1:T(8,128)(2,1)}, u32[]{:S(2)}, u32[]{:S(2)}) collective-permute-start(bf16[512,512]{0,1:T(8,128)(2,1)} %convert_element_type.545), channel_id=1, source_target_pairs={{16,0},{17,1},{18,2},{19,3},{20,4},{21,5},{22,6},{23,7},{24,8},{25... | collective-permute-start | bytes 1572872 | tf_op jit(solution)/shard_map/ppermute | solution.py:19
  372.0 81.1 %copy-start.16 = (f32[512,512]{1,0:T(8,128)S(1)}, f32[512,512]{1,0:T(8,128)}, u32[]{:S(2)}) copy-start(f32[512,512]{1,0:T(8,128)} %copy.145) | copy-start | bytes 3145732
  451.9 2.8 collective-permute-start.4
  453.1 36.7 %copy-start.29 = (f32[10,512]{1,0:T(8,128)S(1)}, f32[10,512]{1,0:T(8,128)}, u32[]{:S(2)}) copy-start(f32[10,512]{1,0:T(8,128)} %copy-done.28) | copy-start | bytes 61444
  453.1 36.7 %copy-start.52 = (f32[10,512]{1,0:T(8,128)S(1)}, f32[10,512]{1,0:T(8,128)}, u32[]{:S(2)}) copy-start(f32[10,512]{1,0:T(8,128)} %param.47) | copy-start | bytes 61444
  454.7 3.7 collective-permute-start.5
  (63 other events, 307.4 us)
Sparse Core Ops, SparseCore 0:
  373.8 78.0 reduce-scatter.1
